TPU v7x, 128 devices: a whole 4x4x4 slice. The times are simulated.
128 devices in a mesh: row: 8 (over z, core), col: 16 (over y, x).
Axes of the slice: x: 4, y: 4, z: 4, core: 2. Of those that a mesh axis runs over, the one named last changes fastest.
Arguments:
- video_scores_in: float32 [131072, 128], P(('col', 'row')), may hold values from -6 to 6
- audio_seed: int32 [131072], P(('row', 'col')), may hold values from 0 to 255
- video_seed: int32 [131072], P(('col', 'row')), may hold values from 0 to 255
- tile_values: bfloat16 [8, 16, 640, 128, 128], P('row', 'col'), may hold values from 0 to 1
- tile_rows: int32 [8, 16, 640], P('row', 'col'), may hold values from 0 to 127, as said below
- tile_cols: int32 [8, 16, 640], P('row', 'col'), may hold values from 0 to 63, as said below
- tile_count: int32 [8, 16], P('row', 'col'), may hold values from 128 to 640, as said below
Outputs:
- audio_scores: float32 [131072, 128], P(('row', 'col'))
- video_scores: float32 [131072, 128], P(('col', 'row'))
Inputs may be any that keep to these rules, and one draw needn't show every extreme that they name: `tile_rows`: every tile row of a cell's row group and every tile column of its column group is named by some live slot of that cell; two slots may name the same tile position, and then both add. `tile_cols`: see tile_rows. `tile_count`: loads differ widely between cells; some cell uses all 640 slots.
All inputs are finite; a program needn't handle non-finite values.
Results may differ from a plain program's by a relative error of at most 0.005.
Values may be sent and summed in bfloat16 or wider, within the bound.
A program may use at most 192 MiB of HBM per device.

v0:
```python
import functools

import jax
import jax.numpy as jnp
from jax import lax
from jax.experimental import pallas as pl
from jax.experimental.pallas import tpu as pltpu
from jax.sharding import PartitionSpec as P

MESH = pl.DeviceIdType.MESH
F32, BF16 = jnp.float32, jnp.bfloat16
VM = pl.BlockSpec(memory_space=pltpu.VMEM)
SM = pl.BlockSpec(memory_space=pltpu.SMEM)
SIDE = 4
OWN = 8
QUART = OWN // 4
T = 128
CHUNK = 32
UNROLL = 16
LIMIT = 67043328
DIRS = (0, 1)


def step(d):
    return 1 if d == 0 else SIDE - 1


class Copies:
    def __init__(self, send, recv):
        self.send, self.recv, self.used, self.open = send, recv, 0, []

    def slot(self):
        self.used += 1
        return self.used - 1

    def start(self, slot, src, dst, to):
        copy = pltpu.make_async_remote_copy(
            src_ref=src,
            dst_ref=dst,
            send_sem=self.send.at[slot],
            recv_sem=self.recv.at[slot],
            device_id=to,
            device_id_type=MESH,
        )
        copy.start()
        self.open.append(copy)
        return copy

    def finish(self):
        for copy in self.open:
            copy.wait_send()


def greet(peers):
    barrier = pltpu.get_barrier_semaphore()
    for peer in peers:
        pl.semaphore_signal(barrier, inc=1, device_id=peer, device_id_type=MESH)
    pl.semaphore_wait(barrier, len(peers))


def plan_kernel(count, rows, cols, by_row, by_col, in_row, in_col):
    slots = rows.shape[1]
    wide = by_row.shape[1]
    lane = lax.broadcasted_iota(jnp.int32, (1, slots), 1)
    live = lane < count[0, 0]
    before = (
        lax.broadcasted_iota(jnp.int32, (slots, slots), 0)
        < lax.broadcasted_iota(jnp.int32, (slots, slots), 1)
    ).astype(BF16)
    below = (
        lax.broadcasted_iota(jnp.int32, (T, T), 0) > lax.broadcasted_iota(jnp.int32, (T, T), 1)
    ).astype(F32)

    def one(key, other, member, index):
        key = jnp.where(live, key, 1023)
        hit = (lax.broadcasted_iota(jnp.int32, (T, slots), 0) == key).astype(F32)
        member[...] = hit[: member.shape[0]].astype(BF16)
        rank = jnp.dot(hit.astype(BF16), before, preferred_element_type=F32)
        rank = jnp.sum(hit * rank, axis=0, keepdims=True)
        size = jnp.sum(hit, axis=1, keepdims=True)
        pairs = jnp.broadcast_to(jnp.floor((size + 1.0) * 0.5), (T, T))
        base = jnp.dot(
            below, pairs, preferred_element_type=F32, precision=lax.Precision.HIGHEST
        )
        start = jnp.sum(hit * base[:, :1], axis=0, keepdims=True)
        place = jnp.where(live, 2.0 * start + rank, -1.0)
        place = jnp.broadcast_to(place, (T, slots)).T
        high = lane // T
        part = lax.broadcasted_iota(jnp.int32, (8, slots), 0)
        facts = jnp.where(part == 0, high, lane - high * T)
        facts = jnp.where(part == 2, other, facts)
        facts = jnp.where(part == 3, 1, facts)
        facts = jnp.where(part == 4, (rank == 0.0).astype(jnp.int32), facts)
        facts = facts.astype(F32).astype(BF16)
        last = (base + pairs - 1.0).T
        row = lax.broadcasted_iota(jnp.int32, (8, T), 0)
        for c in range(wide // T):
            spot = lax.broadcasted_iota(jnp.int32, (slots, T), 1) + c * T
            chosen = (place == spot.astype(F32)).astype(BF16)
            got = jnp.dot(facts, chosen, preferred_element_type=F32)
            tile = got[0:1] * T + got[1:2] + slots * (1.0 - got[3:4])
            value = jnp.where(row == 0, tile, got[2:3])
            value = jnp.where(row == 2, 1.0 - got[4:5], value)
            value = jnp.where(row == 3, last[:8], value)
            index[:, c * T : (c + 1) * T] = value.astype(jnp.int32)

    one(rows[...], cols[...], in_row, by_row)
    one(cols[...], rows[...], in_col, by_col)


def plan(count, rows, cols, n_rows, n_cols):
    slots = rows.shape[1]
    wide = slots + n_rows
    return pl.pallas_call(
        plan_kernel,
        in_specs=[SM, VM, VM],
        out_specs=[VM] * 4,
        out_shape=[
            jax.ShapeDtypeStruct((8, wide), jnp.int32),
            jax.ShapeDtypeStruct((8, wide), jnp.int32),
            jax.ShapeDtypeStruct((n_rows, slots), BF16),
            jax.ShapeDtypeStruct((n_cols, slots), BF16),
        ],
        compiler_params=pltpu.CompilerParams(vmem_limit_bytes=16 * 1024 * 1024),
        name="plan",
    )(count, rows, cols)


def blend(total, mass, seeds):
    labels = (lax.broadcasted_iota(jnp.int32, total.shape, 0) == seeds).astype(F32)
    return total * (0.75 / jnp.sqrt(mass)) + 0.25 * labels


def sweep_kernel(
    by_row, by_col, v_in, tiles_in, in_row, in_col, audio_seeds, video_seeds,
    audio_out, video_out,
    tiles, held, panel, part, full, back, acc, row_sums, col_sums, mass_in, mass_col,
    opp1, plain1, merged1, edge1, sum1, half1, opp2, plain2, merged2, edge2,
    mass_far, mass_edge, mass_sum, mass_hop, mass_far2, mass_edge2, mass_hop2,
    swap, total, half, opp, plain, merged, edge,
    r_swap, r_tot, r_far, r_edge, r_hop,
    send, recv, load,
):
    slots = tiles_in.shape[0]
    n_chunks = slots // CHUNK
    n_cols = panel.shape[0]
    row_id, col_id = lax.axis_index("row"), lax.axis_index("col")
    core = lax.rem(row_id, 2)
    pos = {"y": col_id // SIDE, "x": lax.rem(col_id, SIDE), "z": row_id // 2}
    y, x, z = pos["y"], pos["x"], pos["z"]

    def at(axis, k):
        return lax.rem(pos[axis] + k, SIDE)

    def peer(axis, d):
        if axis == "y":
            return {"col": at("y", step(d)) * SIDE + x}
        if axis == "x":
            return {"col": y * SIDE + at("x", step(d))}
        return {"row": at("z", step(d)) * 2 + core}

    mate = {"row": z * 2 + 1 - core}
    copies = Copies(send, recv)

    def start(src, dst, to):
        return copies.start(copies.slot(), src, dst, to)

    loads = []
    for i in range(n_chunks):
        span = pl.ds(i * CHUNK, CHUNK)
        copy = pltpu.make_async_copy(tiles_in.at[span], tiles.at[span], load.at[i])
        copy.start()
        loads.append(copy)
    tiles[slots] = jnp.zeros((T, T), BF16)

    panel[pl.ds(row_id * OWN, OWN)] = v_in[...].astype(BF16)
    greet([peer(axis, d) for axis in "xyz" for d in DIRS] + [mate])

    def push_video(index, first, size, to):
        ref = panel.at[pl.ds(index * OWN + first, size)]
        return start(ref, ref, to)

    def tile_sums(chunks):
        for i in chunks:
            loads[i].wait()

        @pl.loop(chunks[0], chunks[-1] + 1)
        def _(i):
            sums = lax.dot_general(
                jnp.ones((8, T), BF16),
                tiles[pl.ds(i * CHUNK, CHUNK)].reshape(CHUNK * T, T),
                (((1,), (1,)), ((), ())),
                preferred_element_type=F32,
            )
            for s in range(CHUNK):
                row_sums[pl.ds(i * CHUNK + s, 1)] = sums[0:1, s * T : (s + 1) * T]
                col_sums[pl.ds(i * CHUNK + s, 1)] = jnp.sum(
                    tiles[i * CHUNK + s].astype(F32), axis=0, keepdims=True
                )

    cut = (n_chunks * 9 // 20, n_chunks * 15 // 20)
    hop = [push_video(row_id, 0, OWN, peer("z", d)) for d in DIRS]
    mates = [push_video(row_id, 0, OWN, mate)]
    tile_sums(range(0, cut[0]))
    far = []
    for d in DIRS:
        index = at("z", step(1 - d)) * 2 + core
        hop[d].wait_recv()
        far.append(push_video(index, d * OWN // 2, OWN // 2, peer("z", d)))
        mates.append(push_video(index, 0, OWN, mate))
    tile_sums(range(cut[0], cut[1]))
    for d in DIRS:
        far[d].wait_recv()
        mates.append(push_video(at("z", 2) * 2 + core, d * OWN // 2, OWN // 2, mate))
    tile_sums(range(cut[1], n_chunks))

    def gathered(member, sums):
        value = sums[pl.ds(0, slots)]
        upper = value.astype(BF16)
        lower = (value - upper.astype(F32)).astype(BF16)
        return jnp.dot(member[...], upper, preferred_element_type=F32) + jnp.dot(
            member[...], lower, preferred_element_type=F32
        )

    mass_in[...] = gathered(in_row, row_sums).reshape(mass_in.shape)
    mass_col[...] = gathered(in_col, col_sums).reshape(mass_col.shape)

    c_far = start(mass_in.at[:, at("x", 2)], mass_far, peer("x", 0))
    c_hop = start(mass_in.at[:, at("x", 3)], mass_hop.at[1], peer("x", 1))
    r_mate = start(mass_col.at[:, 1 - core], r_swap, mate)
    for copy in mates:
        copy.wait_recv()

    def products(index, count, left, right):
        acc[...] = jnp.zeros_like(acc)

        @pl.loop(0, count // UNROLL)
        def _(i):
            prods = []
            for u in range(UNROLL):
                g = (i * UNROLL + u) * 2
                a, b = (index[0, g], index[1, g]), (index[0, g + 1], index[1, g + 1])
                prods.append(
                    jnp.dot(
                        jnp.concatenate([left(*a), left(*b)], axis=1),
                        jnp.concatenate([right(*a), right(*b)], axis=0),
                        preferred_element_type=F32,
                    )
                )
            value = acc[...]
            for u in range(UNROLL):
                g = i * UNROLL + u
                value = value * index[2, g * 2].astype(F32) + prods[u]
                held[g] = value.astype(BF16)
            acc[...] = value

    products(by_row, held.shape[0], lambda t, c: tiles[t], lambda t, c: panel[c])

    @pl.loop(0, SIDE * SIDE)
    def _(o):
        for j in range(OWN):
            part[o // SIDE, lax.rem(o, SIDE), j] = held[by_row[3, o * OWN + j]]

    halves = (("x", "y"), ("y", "x"))

    def tiles_of(h, d):
        return pl.ds((2 * h + d) * QUART, QUART)

    def unit(h, index, d):
        return part.at[:, index, tiles_of(h, d)] if h == 0 else part.at[index, :, tiles_of(h, d)]

    c_opp, c_plain, c_merged = {}, {}, {}
    both = [(h, d) for d in DIRS for h in (0, 1)]
    for h, d in both:
        axis = halves[h][0]
        c_opp[h, d] = start(unit(h, at(axis, 2), d), opp1.at[h, d], peer(axis, d))
    for h, d in both:
        axis = halves[h][0]
        c_plain[h, d] = start(
            unit(h, at(axis, step(d)), 1 - d), plain1.at[h, d], peer(axis, d)
        )

    c_far.wait_recv()
    mass_edge[...] = mass_far[...] + mass_in[:, at("x", 1)]
    c_merge = start(mass_edge, mass_hop.at[0], peer("x", 0))
    r_mate.wait_recv()
    r_tot[...] = mass_col[:, core] + r_swap[...]
    r_c_far = start(r_tot.at[at("z", 2)], r_far, peer("z", 0))
    r_c_hop = start(r_tot.at[at("z", 3)], r_hop.at[1], peer("z", 1))

    for h, d in both:
        axis = halves[h][0]
        index = at(axis, step(d))
        c_opp[h, d].wait_recv()
        mine = unit(h, index, d)

        @pl.loop(0, SIDE)
        def _(k):
            edge1[h, d, k] = (mine[k].astype(F32) + opp1[h, d, k].astype(F32)).astype(BF16)

        c_merged[h, d] = start(edge1.at[h, d], merged1.at[h, d], peer(axis, d))

    c_hop.wait_recv()
    c_merge.wait_recv()
    mass_sum[...] = mass_in[:, x] + mass_hop[0] + mass_hop[1]
    c_far = start(mass_sum.at[at("y", 2)], mass_far2, peer("y", 0))
    c_hop = start(mass_sum.at[at("y", 3)], mass_hop2.at[1], peer("y", 1))
    r_c_far.wait_recv()
    r_edge[...] = r_far[...] + r_tot[at("z", 1)]
    r_c_merge = start(r_edge, r_hop.at[0], peer("z", 0))

    for h, d in both:
        c_plain[h, 1 - d].wait_recv()
        c_merged[h, d].wait_recv()
        mine = unit(h, pos[halves[h][0]], d)

        @pl.loop(0, SIDE)
        def _(k):
            value = (
                mine[k].astype(F32)
                + merged1[h, d, k].astype(F32)
                + plain1[h, 1 - d, k].astype(F32)
            )
            sum1[h, d, k] = value
            half1[h, d, k] = value.astype(BF16)

        axis = halves[h][1]
        c_opp[h, d] = start(half1.at[h, d, at(axis, 2)], opp2.at[h, d], peer(axis, d))
        c_plain[h, 1 - d] = start(
            half1.at[h, d, at(axis, step(1 - d))], plain2.at[h, 1 - d], peer(axis, 1 - d)
        )

    c_far.wait_recv()
    mass_edge2[...] = mass_far2[...] + mass_sum[at("y", 1)]
    c_merge = start(mass_edge2, mass_hop2.at[0], peer("y", 0))

    for h, d in both:
        axis = halves[h][1]
        c_opp[h, d].wait_recv()
        edge2[h, d] = (sum1[h, d, at(axis, step(d))] + opp2[h, d].astype(F32)).astype(BF16)
        c_merged[h, d] = start(edge2.at[h, d], merged2.at[h, d], peer(axis, d))

    c_hop.wait_recv()
    c_merge.wait_recv()
    mass = mass_sum[y] + mass_hop2[0] + mass_hop2[1]
    r_c_hop.wait_recv()
    r_c_merge.wait_recv()
    mass_video = r_tot[z] + r_hop[0] + r_hop[1]

    def spot(h, k, u):
        return (k * SIDE + u) * OWN if h == 0 else (u * SIDE + k) * OWN

    for h, d in both:
        axis = halves[h][1]
        c_plain[h, 1 - d].wait_recv()
        c_merged[h, d].wait_recv()
        for i in range(QUART):
            t = (2 * h + d) * QUART + i
            value = (
                sum1[h, d, pos[axis], i]
                + merged2[h, d, i].astype(F32)
                + plain2[h, 1 - d, i].astype(F32)
            )
            scores = blend(value.T, mass[t : t + 1], audio_seeds[t : t + 1])
            audio_out[t] = scores
            full[col_id * OWN + t] = scores.astype(BF16)

    def push(h, k, u, d, axis, way):
        if d is None:
            span = pl.ds(spot(h, k, u) + 2 * h * QUART, 2 * QUART)
        else:
            span = pl.ds(spot(h, k, u) + (2 * h + d) * QUART, QUART)
        ref = full.at[span]
        return start(ref, ref, peer(axis, way))

    c_a, c_af, c_b, c_bf = {}, {}, {}, {}
    for h in (0, 1):
        second, first = halves[h]
        for d in DIRS:
            c_a[h, d] = push(h, pos[first], pos[second], None, first, d)
    for h in (0, 1):
        second, first = halves[h]
        for d in DIRS:
            c_b[h, "own", d] = push(h, pos[first], pos[second], None, second, d)
    for h, d in both:
        second, first = halves[h]
        c_a[h, d].wait_recv()
        k = at(first, step(1 - d))
        c_af[h, d] = push(h, k, pos[second], d, first, d)
        for e in DIRS:
            c_b[h, d, e] = push(h, k, pos[second], None, second, e)
    for h, d in both:
        second, first = halves[h]
        c_b[h, "own", d].wait_recv()
        c_bf[h, "own", d] = push(h, pos[first], at(second, step(1 - d)), d, second, d)
    for h, d in both:
        second, first = halves[h]
        c_af[h, d].wait_recv()
        for e in DIRS:
            c_b[h, "far", d, e] = push(h, at(first, 2), pos[second], d, second, e)
    for h, e in both:
        second, first = halves[h]
        for d in DIRS:
            c_b[h, d, e].wait_recv()
            c_bf[h, d, e] = push(
                h, at(first, step(1 - d)), at(second, step(1 - e)), e, second, e
            )
    for h, e in both:
        second, first = halves[h]
        c_b[h, "far", e, e].wait_recv()
        c_bf[h, "far", e] = push(h, at(first, 2), at(second, step(1 - e)), e, second, e)
    for h, d in both:
        c_b[h, "far", d, 1 - d].wait_recv()
    for copy in c_bf.values():
        copy.wait_recv()

    products(
        by_col, (slots + n_cols) // 2, lambda t, r: full[r], lambda t, r: tiles[t]
    )

    @pl.loop(0, 2 * SIDE)
    def _(o):
        for j in range(OWN):
            back[o // 2, lax.rem(o, 2), j] = held[by_col[3, o * OWN + j]]

    piece = [pl.ds(0, OWN // 2), pl.ds(OWN // 2, OWN // 2)]
    order = (2, 1, 3, 0)
    c_swap = [
        start(back.at[at("z", k), 1 - core], swap.at[i], mate) for i, k in enumerate(order)
    ]

    def add_mate(i):
        c_swap[i].wait_recv()
        index = at("z", order[i])

        @pl.loop(0, OWN)
        def _(t):
            value = back[index, core, t].astype(F32) + swap[i, t].astype(F32)
            total[i, t] = value
            half[i, t] = value.astype(BF16)

    add_mate(0)
    c_opp = [start(half.at[0, piece[d]], opp.at[d], peer("z", d)) for d in DIRS]
    c_plain = []
    for d in DIRS:
        add_mate(1 + d)
        c_plain.append(start(half.at[1 + d, piece[1 - d]], plain.at[d], peer("z", d)))
    add_mate(3)
    c_merged = []
    for d in DIRS:
        c_opp[d].wait_recv()

        @pl.loop(0, OWN // 2)
        def _(t):
            edge[d, t] = (total[1 + d, d * (OWN // 2) + t] + opp[d, t].astype(F32)).astype(BF16)

        c_merged.append(start(edge.at[d], merged.at[d], peer("z", d)))
    for d in DIRS:
        c_plain[1 - d].wait_recv()
        c_merged[d].wait_recv()
        for i in range(OWN // 2):
            t = d * (OWN // 2) + i
            value = total[3, t] + merged[d, i].astype(F32) + plain[1 - d, i].astype(F32)
            video_out[t] = blend(value, mass_video[t : t + 1], video_seeds[t : t + 1])
    copies.finish()


def sweep(by_row, by_col, v, tiles, in_row, in_col, audio_seeds, video_seeds):
    slots = tiles.shape[0]
    n_rows, n_cols = in_row.shape[0], in_col.shape[0]
    unit = (2, 2, SIDE, QUART, T, T)
    small = (2, 2, QUART, T, T)
    quad = (2, OWN // 2, T, T)
    count = 9 + 6 + 4 + 24 + 44 + 10
    scratch = [
        pltpu.VMEM((slots + 1, T, T), BF16),
        pltpu.VMEM(((slots + n_rows) // 2, T, T), BF16),
        pltpu.VMEM((n_cols, T, T), BF16),
        pltpu.VMEM((SIDE, SIDE, OWN, T, T), BF16),
        pltpu.VMEM((n_rows, T, T), BF16),
        pltpu.VMEM((SIDE, 2, OWN, T, T), BF16),
        pltpu.VMEM((T, T), F32),
        pltpu.VMEM((slots, T), F32),
        pltpu.VMEM((slots, T), F32),
        pltpu.VMEM((SIDE, SIDE, OWN, T), F32),
        pltpu.VMEM((SIDE, 2, OWN, T), F32),
        pltpu.VMEM(unit, BF16),
        pltpu.VMEM(unit, BF16),
        pltpu.VMEM(unit, BF16),
        pltpu.VMEM(unit, BF16),
        pltpu.VMEM(unit, F32),
        pltpu.VMEM(unit, BF16),
        pltpu.VMEM(small, BF16),
        pltpu.VMEM(small, BF16),
        pltpu.VMEM(small, BF16),
        pltpu.VMEM(small, BF16),
        pltpu.VMEM((SIDE, OWN, T), F32),
        pltpu.VMEM((SIDE, OWN, T), F32),
        pltpu.VMEM((SIDE, OWN, T), F32),
        pltpu.VMEM((2, SIDE, OWN, T), F32),
        pltpu.VMEM((OWN, T), F32),
        pltpu.VMEM((OWN, T), F32),
        pltpu.VMEM((2, OWN, T), F32),
        pltpu.VMEM((SIDE, OWN, T, T), BF16),
        pltpu.VMEM((SIDE, OWN, T, T), F32),
        pltpu.VMEM((SIDE, OWN, T, T), BF16),
        pltpu.VMEM(quad, BF16),
        pltpu.VMEM(quad, BF16),
        pltpu.VMEM(quad, BF16),
        pltpu.VMEM(quad, BF16),
        pltpu.VMEM((SIDE, OWN, T), F32),
        pltpu.VMEM((SIDE, OWN, T), F32),
        pltpu.VMEM((OWN, T), F32),
        pltpu.VMEM((OWN, T), F32),
        pltpu.VMEM((2, OWN, T), F32),
        pltpu.SemaphoreType.DMA((count,)),
        pltpu.SemaphoreType.DMA((count,)),
        pltpu.SemaphoreType.DMA((slots // CHUNK,)),
    ]
    return pl.pallas_call(
        sweep_kernel,
        in_specs=[SM, SM, VM, pl.BlockSpec(memory_space=pl.ANY), VM, VM, VM, VM],
        out_specs=[VM, VM],
        out_shape=[jax.ShapeDtypeStruct((OWN, T, T), F32)] * 2,
        scratch_shapes=scratch,
        compiler_params=pltpu.CompilerParams(
            collective_id=0, has_side_effects=True, vmem_limit_bytes=LIMIT
        ),
        name="sweep",
    )(by_row, by_col, v, tiles, in_row, in_col, audio_seeds, video_seeds)


def turn_kernel(a, b, a_out, b_out):
    for t in range(OWN):
        a_out[t] = a[t].T
        b_out[t] = b[t].T


def turn(a, b):
    return pl.pallas_call(
        turn_kernel,
        in_specs=[VM, VM],
        out_specs=[VM, VM],
        out_shape=[jax.ShapeDtypeStruct(a.shape, F32)] * 2,
        name="turn",
    )(a, b)


def body(video_scores_in, audio_seed, video_seed, tile_values, tile_rows, tile_cols, tile_count):
    n_rows, n_cols = SIDE * SIDE * OWN, 2 * SIDE * OWN
    by_row, by_col, in_row, in_col = plan(
        tile_count, tile_rows[0], tile_cols[0], n_rows, n_cols
    )
    audio, video = sweep(
        by_row,
        by_col,
        video_scores_in.reshape(OWN, T, T),
        tile_values[0, 0],
        in_row,
        in_col,
        audio_seed.reshape(OWN, T),
        video_seed.reshape(OWN, T),
    )
    audio, video = turn(audio, video)
    return (audio.reshape(OWN * T, T), video.reshape(OWN * T, T))


def solution(mesh):
    in_specs = (
        P(("col", "row"), None),
        P(("row", "col")),
        P(("col", "row")),
        P("row", "col", None, None, None),
        P("row", "col", None),
        P("row", "col", None),
        P("row", "col"),
    )
    out_specs = (P(("row", "col"), None), P(("col", "row"), None))
    return jax.shard_map(body, mesh=mesh, in_specs=in_specs, out_specs=out_specs, check_vma=False)
```

profile of v0, /device:TPU:1, one launch (start us, length us, event | category | flops | bytes accessed | tf_op | source)
XLA Modules:
  0.0 117.9 jit_solution(1466860534991996609)
XLA Ops:
  1.3 0.0 copy-start.4
  1.3 0.7 copy-done.4
  2.0 0.0 copy-start.5
  2.0 0.7 copy-done.5
  2.6 1.7 %plan.1 = (s32[8,768]{1,0:T(8,128)S(1)}, s32[8,768]{1,0:T(8,128)S(1)}, bf16[128,640]{1,0:T(8,128)(2,1)S(1)}, bf16[64,640]{1,0:T(8,128)(2,1)S(1)}) custom-call(s32[1,1]{1,0:T(1,128)S(6)} %copy.9.count, s32[1,640]{1,0:T(1,128)S(1)} %bitcast.8, s32[1,640]{1,0:T(1,128)S(1)} %bitcast.9), custom_call_target="tpu_custom_call" | custom-call | tf_op jit(solution)/shard_map/plan/pallas_call | solution.py:114
  4.3 0.0 copy-start
  4.3 0.7 copy-done
  5.0 0.0 copy-start.1
  5.0 0.6 copy-done.1
  5.6 0.0 copy-start.2
  5.6 0.6 copy-done.2
  6.2 0.0 copy-start.3
  6.2 0.6 copy-done.3
  6.8 108.5 %sweep.1 = (f32[8,128,128]{2,1,0:T(8,128)}, f32[8,128,128]{2,1,0:T(8,128)}) custom-call(s32[8,768]{1,0:T(8,128)} %copy-done.2, s32[8,768]{1,0:T(8,128)} %copy-done.3, f32[8,128,128]{2,1,0:T(8,128)} %bitcast.11, bf16[640,128,128]{2,1,0:T(8,128)(2,1)} %bitcast.10, bf16[128,640]{1,0:T(8,128)(2,1)} %copy-done, bf16[64,640]{1,0:T(8,128)(2,1)} %copy-done.1, ...), custom_call_target="tpu_custom_call" | custom-call | tf_op jit(solution)/shard_map/sweep/pallas_call | solution.py:520
  115.4 2.5 %turn.1 = (f32[8,128,128]{2,1,0:T(8,128)}, f32[8,128,128]{2,1,0:T(8,128)}) custom-call(f32[8,128,128]{2,1,0:T(8,128)} %get-tuple-element.14.a, f32[8,128,128]{2,1,0:T(8,128)} %get-tuple-element.15.b), custom_call_target="tpu_custom_call" | custom-call | tf_op jit(solution)/shard_map/turn/pallas_call | solution.py:540
Async XLA Ops:
  1.3 0.7 copy-start.4
  2.0 0.7 copy-start.5
  4.3 0.7 copy-start
  5.0 0.6 copy-start.1
  5.6 0.6 copy-start.2
  6.2 0.6 copy-start.3
where the time goes:
time: 118 us
  Pallas kernels  113 us (96%)
  local copies, waits for them, and re-layouts  3.88 us (3%)
  between operations  1.31 us (1%)
    pallas_call x1, Pallas kernels, sweep(): pl.pallas_call(sweep_kernel, in_specs=[SM, SM, VM, pl.BlockSpec(memory_sp...  109 us
    unnamed x12, local copies, waits for them, and re-layouts  3.88 us
    pallas_call x1, Pallas kernels, turn(): pl.pallas_call(turn_kernel, in_specs=[VM, VM], out_specs=[VM, VM], out_sh...  2.5 us

commit v1 on v0

--- a/solution.py
+++ b/solution.py
@@ -1,5 +1,3 @@
-import functools
-
 import jax
 import jax.numpy as jnp
 from jax import lax
@@ -10,7 +8,6 @@
 MESH = pl.DeviceIdType.MESH
 F32, BF16 = jnp.float32, jnp.bfloat16
 VM = pl.BlockSpec(memory_space=pltpu.VMEM)
-SM = pl.BlockSpec(memory_space=pltpu.SMEM)
 SIDE = 4
 OWN = 8
 QUART = OWN // 4
@@ -19,6 +16,7 @@
 UNROLL = 16
 LIMIT = 67043328
 DIRS = (0, 1)
+REL = (2, 1, 3, 0)
 
 
 def step(d):
@@ -58,7 +56,7 @@
     pl.semaphore_wait(barrier, len(peers))
 
 
-def plan_kernel(count, rows, cols, by_row, by_col, in_row, in_col):
+def sort_slots(count, rows, cols, by_row, by_col, in_row, in_col):
     slots = rows.shape[1]
     wide = by_row.shape[1]
     lane = lax.broadcasted_iota(jnp.int32, (1, slots), 1)
@@ -92,7 +90,7 @@
         facts = jnp.where(part == 3, 1, facts)
         facts = jnp.where(part == 4, (rank == 0.0).astype(jnp.int32), facts)
         facts = facts.astype(F32).astype(BF16)
-        last = (base + pairs - 1.0).T
+        last = jnp.maximum(base + pairs - 1.0, 0.0).T
         row = lax.broadcasted_iota(jnp.int32, (8, T), 0)
         for c in range(wide // T):
             spot = lax.broadcasted_iota(jnp.int32, (slots, T), 1) + c * T
@@ -108,20 +106,42 @@
     one(cols[...], rows[...], in_col, by_col)
 
 
+def plan_kernel(count_in, rows_in, cols_in, *refs):
+    outs, count, rows, cols, found, sems = refs[:4], refs[4], refs[5], refs[6], refs[7:11], refs[11]
+    pairs = [(count_in, count), (rows_in, rows), (cols_in, cols), *zip(found, outs)]
+    moves = [pltpu.make_async_copy(a, b, sems.at[i]) for i, (a, b) in enumerate(pairs)]
+    for move in moves[:3]:
+        move.start()
+    for move in moves[:3]:
+        move.wait()
+    sort_slots(count, rows, cols, *found)
+    for move in moves[3:]:
+        move.start()
+    for move in moves[3:]:
+        move.wait()
+
+
 def plan(count, rows, cols, n_rows, n_cols):
     slots = rows.shape[1]
     wide = slots + n_rows
+    anywhere = pl.BlockSpec(memory_space=pl.ANY)
+    hbm = pl.BlockSpec(memory_space=pltpu.HBM)
+    kinds = [
+        ((8, wide), jnp.int32), ((8, wide), jnp.int32), ((n_rows, slots), BF16), ((n_cols, slots), BF16)
+    ]
     return pl.pallas_call(
         plan_kernel,
-        in_specs=[SM, VM, VM],
-        out_specs=[VM] * 4,
-        out_shape=[
-            jax.ShapeDtypeStruct((8, wide), jnp.int32),
-            jax.ShapeDtypeStruct((8, wide), jnp.int32),
-            jax.ShapeDtypeStruct((n_rows, slots), BF16),
-            jax.ShapeDtypeStruct((n_cols, slots), BF16),
+        in_specs=[anywhere] * 3,
+        out_specs=[hbm] * 4,
+        out_shape=[jax.ShapeDtypeStruct(*kind) for kind in kinds],
+        scratch_shapes=[
+            pltpu.SMEM((1, 1), jnp.int32),
+            pltpu.VMEM((1, slots), jnp.int32),
+            pltpu.VMEM((1, slots), jnp.int32),
+            *[pltpu.VMEM(*kind) for kind in kinds],
+            pltpu.SemaphoreType.DMA((7,)),
         ],
-        compiler_params=pltpu.CompilerParams(vmem_limit_bytes=16 * 1024 * 1024),
+        compiler_params=pltpu.CompilerParams(vmem_limit_bytes=60 * 1024 * 1024),
         name="plan",
     )(count, rows, cols)
 
@@ -132,14 +152,16 @@
 
 
 def sweep_kernel(
-    by_row, by_col, v_in, tiles_in, in_row, in_col, audio_seeds, video_seeds,
+    by_row_in, by_col_in, in_row_in, in_col_in, v_in, tiles_in, audio_seeds_in, video_seeds_in,
     audio_out, video_out,
     tiles, held, panel, part, full, back, acc, row_sums, col_sums, mass_in, mass_col,
-    opp1, plain1, merged1, edge1, sum1, half1, opp2, plain2, merged2, edge2,
+    by_row, by_col, in_row, in_col,
+    v, audio_seeds, video_seeds, audio, video,
+    opp1, plain1, merged1, edge1, half1, sum1, own1, opp2, plain2, merged2, edge2,
     mass_far, mass_edge, mass_sum, mass_hop, mass_far2, mass_edge2, mass_hop2,
     swap, total, half, opp, plain, merged, edge,
     r_swap, r_tot, r_far, r_edge, r_hop,
-    send, recv, load,
+    send, recv, load, aux,
 ):
     slots = tiles_in.shape[0]
     n_chunks = slots // CHUNK
@@ -165,6 +187,15 @@
     def start(src, dst, to):
         return copies.start(copies.slot(), src, dst, to)
 
+    def local(src, dst, slot):
+        copy = pltpu.make_async_copy(src, dst, aux.at[slot])
+        copy.start()
+        return copy
+
+    v_load = local(v_in, v, 0)
+    index_loads = [local(by_row_in, by_row, 1), local(by_col_in, by_col, 2)]
+    member_loads = [local(in_row_in, in_row, 3), local(in_col_in, in_col, 6)]
+    seed_loads = [local(audio_seeds_in, audio_seeds, 4), local(video_seeds_in, video_seeds, 5)]
     loads = []
     for i in range(n_chunks):
         span = pl.ds(i * CHUNK, CHUNK)
@@ -173,7 +204,8 @@
         loads.append(copy)
     tiles[slots] = jnp.zeros((T, T), BF16)
 
-    panel[pl.ds(row_id * OWN, OWN)] = v_in[...].astype(BF16)
+    v_load.wait()
+    panel[pl.ds(row_id * OWN, OWN)] = v[...].astype(BF16)
     greet([peer(axis, d) for axis in "xyz" for d in DIRS] + [mate])
 
     def push_video(index, first, size, to):
@@ -198,7 +230,7 @@
                     tiles[i * CHUNK + s].astype(F32), axis=0, keepdims=True
                 )
 
-    cut = (n_chunks * 9 // 20, n_chunks * 15 // 20)
+    cut = (n_chunks * 7 // 20, n_chunks * 14 // 20)
     hop = [push_video(row_id, 0, OWN, peer("z", d)) for d in DIRS]
     mates = [push_video(row_id, 0, OWN, mate)]
     tile_sums(range(0, cut[0]))
@@ -222,19 +254,31 @@
             member[...], lower, preferred_element_type=F32
         )
 
+    for copy in member_loads:
+        copy.wait()
     mass_in[...] = gathered(in_row, row_sums).reshape(mass_in.shape)
     mass_col[...] = gathered(in_col, col_sums).reshape(mass_col.shape)
 
     c_far = start(mass_in.at[:, at("x", 2)], mass_far, peer("x", 0))
     c_hop = start(mass_in.at[:, at("x", 3)], mass_hop.at[1], peer("x", 1))
     r_mate = start(mass_col.at[:, 1 - core], r_swap, mate)
+    for copy in index_loads:
+        copy.wait()
     for copy in mates:
         copy.wait_recv()
 
-    def products(index, count, left, right):
+    def products(index, pairs, left, right, between=()):
         acc[...] = jnp.zeros_like(acc)
-
-        @pl.loop(0, count // UNROLL)
+        steps, done = pairs // UNROLL, 0
+        for n, act in enumerate(between):
+            until = steps * (n + 1) // (len(between) + 1)
+            some_products(index, done, until, left, right)
+            act()
+            done = until
+        some_products(index, done, steps, left, right)
+
+    def some_products(index, first, last, left, right):
+        @pl.loop(first, last)
         def _(i):
             prods = []
             for u in range(UNROLL):
@@ -254,7 +298,39 @@
                 held[g] = value.astype(BF16)
             acc[...] = value
 
-    products(by_row, held.shape[0], lambda t, c: tiles[t], lambda t, c: panel[c])
+    moves = {"far": c_far, "hop": c_hop}
+
+    def mass_1():
+        moves["far"].wait_recv()
+        mass_edge[...] = mass_far[...] + mass_in[:, at("x", 1)]
+        moves["merge"] = start(mass_edge, mass_hop.at[0], peer("x", 0))
+        r_mate.wait_recv()
+        r_tot[...] = mass_col[:, core] + r_swap[...]
+        moves["r_far"] = start(r_tot.at[at("z", 2)], r_far, peer("z", 0))
+        moves["r_hop"] = start(r_tot.at[at("z", 3)], r_hop.at[1], peer("z", 1))
+
+    def mass_2():
+        moves["hop"].wait_recv()
+        moves["merge"].wait_recv()
+        mass_sum[...] = mass_in[:, x] + mass_hop[0] + mass_hop[1]
+        moves["far"] = start(mass_sum.at[at("y", 2)], mass_far2, peer("y", 0))
+        moves["hop"] = start(mass_sum.at[at("y", 3)], mass_hop2.at[1], peer("y", 1))
+        moves["r_far"].wait_recv()
+        r_edge[...] = r_far[...] + r_tot[at("z", 1)]
+        moves["r_merge"] = start(r_edge, r_hop.at[0], peer("z", 0))
+
+    def mass_3():
+        moves["far"].wait_recv()
+        mass_edge2[...] = mass_far2[...] + mass_sum[at("y", 1)]
+        moves["merge"] = start(mass_edge2, mass_hop2.at[0], peer("y", 0))
+
+    products(
+        by_row,
+        held.shape[0],
+        lambda t, c: tiles[t],
+        lambda t, c: panel[c],
+        (mass_1, mass_2, mass_3),
+    )
 
     @pl.loop(0, SIDE * SIDE)
     def _(o):
@@ -266,103 +342,91 @@
     def tiles_of(h, d):
         return pl.ds((2 * h + d) * QUART, QUART)
 
-    def unit(h, index, d):
-        return part.at[:, index, tiles_of(h, d)] if h == 0 else part.at[index, :, tiles_of(h, d)]
+    both = [(h, d) for d in DIRS for h in (0, 1)]
+
+    def cell(h, place, i, d):
+        k = at(halves[h][1], REL[i])
+        return part.at[k, place, tiles_of(h, d)] if h == 0 else part.at[place, k, tiles_of(h, d)]
 
     c_opp, c_plain, c_merged = {}, {}, {}
-    both = [(h, d) for d in DIRS for h in (0, 1)]
-    for h, d in both:
-        axis = halves[h][0]
-        c_opp[h, d] = start(unit(h, at(axis, 2), d), opp1.at[h, d], peer(axis, d))
-    for h, d in both:
-        axis = halves[h][0]
-        c_plain[h, d] = start(
-            unit(h, at(axis, step(d)), 1 - d), plain1.at[h, d], peer(axis, d)
+
+    def send_plain(i):
+        for h, d in both:
+            axis = halves[h][0]
+            c_plain[h, d, i] = start(
+                cell(h, at(axis, step(d)), i, 1 - d), plain1.at[h, d, i], peer(axis, d)
+            )
+
+    for i in range(SIDE):
+        for h, d in both:
+            axis = halves[h][0]
+            c_opp[h, d, i] = start(cell(h, at(axis, 2), i, d), opp1.at[h, d, i], peer(axis, d))
+    send_plain(0)
+    for i in range(SIDE):
+        for h, d in both:
+            axis = halves[h][0]
+            c_opp[h, d, i].wait_recv()
+            mine = cell(h, at(axis, step(d)), i, d)
+            edge1[h, d, i] = (mine[...].astype(F32) + opp1[h, d, i].astype(F32)).astype(BF16)
+            c_merged[h, d, i] = start(edge1.at[h, d, i], merged1.at[h, d, i], peer(axis, d))
+        if i + 1 < SIDE:
+            send_plain(i + 1)
+
+    def first_sum(h, d, i):
+        c_plain[h, 1 - d, i].wait_recv()
+        c_merged[h, d, i].wait_recv()
+        mine = cell(h, pos[halves[h][0]], i, d)
+        return (
+            mine[...].astype(F32)
+            + merged1[h, d, i].astype(F32)
+            + plain1[h, 1 - d, i].astype(F32)
         )
 
-    c_far.wait_recv()
-    mass_edge[...] = mass_far[...] + mass_in[:, at("x", 1)]
-    c_merge = start(mass_edge, mass_hop.at[0], peer("x", 0))
-    r_mate.wait_recv()
-    r_tot[...] = mass_col[:, core] + r_swap[...]
-    r_c_far = start(r_tot.at[at("z", 2)], r_far, peer("z", 0))
-    r_c_hop = start(r_tot.at[at("z", 3)], r_hop.at[1], peer("z", 1))
-
-    for h, d in both:
-        axis = halves[h][0]
-        index = at(axis, step(d))
+    for h, d in both:
+        half1[h, d, 0] = first_sum(h, d, 0).astype(BF16)
+        axis = halves[h][1]
+        c_opp[h, d] = start(half1.at[h, d, 0], opp2.at[h, d], peer(axis, d))
+    for e in DIRS:
+        for h, d in both:
+            value = first_sum(h, d, 1 + e)
+            if d == e:
+                sum1[h, d] = value
+            else:
+                half1[h, d, 1] = value.astype(BF16)
+                c_plain[h, e] = start(
+                    half1.at[h, d, 1], plain2.at[h, e], peer(halves[h][1], e)
+                )
+    for h, d in both:
         c_opp[h, d].wait_recv()
-        mine = unit(h, index, d)
-
-        @pl.loop(0, SIDE)
-        def _(k):
-            edge1[h, d, k] = (mine[k].astype(F32) + opp1[h, d, k].astype(F32)).astype(BF16)
-
-        c_merged[h, d] = start(edge1.at[h, d], merged1.at[h, d], peer(axis, d))
-
-    c_hop.wait_recv()
-    c_merge.wait_recv()
-    mass_sum[...] = mass_in[:, x] + mass_hop[0] + mass_hop[1]
-    c_far = start(mass_sum.at[at("y", 2)], mass_far2, peer("y", 0))
-    c_hop = start(mass_sum.at[at("y", 3)], mass_hop2.at[1], peer("y", 1))
-    r_c_far.wait_recv()
-    r_edge[...] = r_far[...] + r_tot[at("z", 1)]
-    r_c_merge = start(r_edge, r_hop.at[0], peer("z", 0))
-
-    for h, d in both:
-        c_plain[h, 1 - d].wait_recv()
-        c_merged[h, d].wait_recv()
-        mine = unit(h, pos[halves[h][0]], d)
-
-        @pl.loop(0, SIDE)
-        def _(k):
-            value = (
-                mine[k].astype(F32)
-                + merged1[h, d, k].astype(F32)
-                + plain1[h, 1 - d, k].astype(F32)
-            )
-            sum1[h, d, k] = value
-            half1[h, d, k] = value.astype(BF16)
-
-        axis = halves[h][1]
-        c_opp[h, d] = start(half1.at[h, d, at(axis, 2)], opp2.at[h, d], peer(axis, d))
-        c_plain[h, 1 - d] = start(
-            half1.at[h, d, at(axis, step(1 - d))], plain2.at[h, 1 - d], peer(axis, 1 - d)
-        )
-
-    c_far.wait_recv()
-    mass_edge2[...] = mass_far2[...] + mass_sum[at("y", 1)]
-    c_merge = start(mass_edge2, mass_hop2.at[0], peer("y", 0))
-
-    for h, d in both:
-        axis = halves[h][1]
-        c_opp[h, d].wait_recv()
-        edge2[h, d] = (sum1[h, d, at(axis, step(d))] + opp2[h, d].astype(F32)).astype(BF16)
-        c_merged[h, d] = start(edge2.at[h, d], merged2.at[h, d], peer(axis, d))
-
-    c_hop.wait_recv()
-    c_merge.wait_recv()
+        edge2[h, d] = (sum1[h, d] + opp2[h, d].astype(F32)).astype(BF16)
+        c_merged[h, d] = start(edge2.at[h, d], merged2.at[h, d], peer(halves[h][1], d))
+    for h, d in both:
+        own1[h, d] = first_sum(h, d, 3)
+
+    moves["hop"].wait_recv()
+    moves["merge"].wait_recv()
     mass = mass_sum[y] + mass_hop2[0] + mass_hop2[1]
-    r_c_hop.wait_recv()
-    r_c_merge.wait_recv()
+    moves["r_hop"].wait_recv()
+    moves["r_merge"].wait_recv()
     mass_video = r_tot[z] + r_hop[0] + r_hop[1]
+    for copy in seed_loads:
+        copy.wait()
 
     def spot(h, k, u):
         return (k * SIDE + u) * OWN if h == 0 else (u * SIDE + k) * OWN
 
     for h, d in both:
-        axis = halves[h][1]
         c_plain[h, 1 - d].wait_recv()
         c_merged[h, d].wait_recv()
         for i in range(QUART):
             t = (2 * h + d) * QUART + i
             value = (
-                sum1[h, d, pos[axis], i]
+                own1[h, d, i]
                 + merged2[h, d, i].astype(F32)
                 + plain2[h, 1 - d, i].astype(F32)
             )
             scores = blend(value.T, mass[t : t + 1], audio_seeds[t : t + 1])
-            audio_out[t] = scores
+            audio[t] = scores
             full[col_id * OWN + t] = scores.astype(BF16)
 
     def push(h, k, u, d, axis, way):
@@ -373,6 +437,7 @@
         ref = full.at[span]
         return start(ref, ref, peer(axis, way))
 
+    audio_store = local(audio, audio_out, 7)
     c_a, c_af, c_b, c_bf = {}, {}, {}, {}
     for h in (0, 1):
         second, first = halves[h]
@@ -461,20 +526,24 @@
         for i in range(OWN // 2):
             t = d * (OWN // 2) + i
             value = total[3, t] + merged[d, i].astype(F32) + plain[1 - d, i].astype(F32)
-            video_out[t] = blend(value, mass_video[t : t + 1], video_seeds[t : t + 1])
+            video[t] = blend(value, mass_video[t : t + 1], video_seeds[t : t + 1])
+    video_store = local(video, video_out, 8)
+    audio_store.wait()
+    video_store.wait()
     copies.finish()
 
 
-def sweep(by_row, by_col, v, tiles, in_row, in_col, audio_seeds, video_seeds):
+def sweep(by_row, by_col, in_row, in_col, v, tiles, audio_seeds, video_seeds):
     slots = tiles.shape[0]
-    n_rows, n_cols = in_row.shape[0], in_col.shape[0]
+    n_rows, n_cols = SIDE * SIDE * OWN, 2 * SIDE * OWN
+    wide = slots + n_rows
     unit = (2, 2, SIDE, QUART, T, T)
     small = (2, 2, QUART, T, T)
     quad = (2, OWN // 2, T, T)
-    count = 9 + 6 + 4 + 24 + 44 + 10
+    copies = 9 + 6 + 4 + 48 + 12 + 44 + 10
     scratch = [
         pltpu.VMEM((slots + 1, T, T), BF16),
-        pltpu.VMEM(((slots + n_rows) // 2, T, T), BF16),
+        pltpu.VMEM((wide // 2, T, T), BF16),
         pltpu.VMEM((n_cols, T, T), BF16),
         pltpu.VMEM((SIDE, SIDE, OWN, T, T), BF16),
         pltpu.VMEM((n_rows, T, T), BF16),
@@ -484,12 +553,22 @@
         pltpu.VMEM((slots, T), F32),
         pltpu.VMEM((SIDE, SIDE, OWN, T), F32),
         pltpu.VMEM((SIDE, 2, OWN, T), F32),
+        pltpu.SMEM((8, wide), jnp.int32),
+        pltpu.SMEM((8, wide), jnp.int32),
+        pltpu.VMEM((n_rows, slots), BF16),
+        pltpu.VMEM((n_cols, slots), BF16),
+        pltpu.VMEM((OWN, T, T), F32),
+        pltpu.VMEM((OWN, T), jnp.int32),
+        pltpu.VMEM((OWN, T), jnp.int32),
+        pltpu.VMEM((OWN, T, T), F32),
+        pltpu.VMEM((OWN, T, T), F32),
         pltpu.VMEM(unit, BF16),
         pltpu.VMEM(unit, BF16),
         pltpu.VMEM(unit, BF16),
         pltpu.VMEM(unit, BF16),
-        pltpu.VMEM(unit, F32),
-        pltpu.VMEM(unit, BF16),
+        pltpu.VMEM((2, 2, 2, QUART, T, T), BF16),
+        pltpu.VMEM(small, F32),
+        pltpu.VMEM(small, F32),
         pltpu.VMEM(small, BF16),
         pltpu.VMEM(small, BF16),
         pltpu.VMEM(small, BF16),
@@ -513,21 +592,23 @@
         pltpu.VMEM((OWN, T), F32),
         pltpu.VMEM((OWN, T), F32),
         pltpu.VMEM((2, OWN, T), F32),
-        pltpu.SemaphoreType.DMA((count,)),
-        pltpu.SemaphoreType.DMA((count,)),
+        pltpu.SemaphoreType.DMA((copies,)),
+        pltpu.SemaphoreType.DMA((copies,)),
         pltpu.SemaphoreType.DMA((slots // CHUNK,)),
+        pltpu.SemaphoreType.DMA((9,)),
     ]
+    anywhere = pl.BlockSpec(memory_space=pl.ANY)
     return pl.pallas_call(
         sweep_kernel,
-        in_specs=[SM, SM, VM, pl.BlockSpec(memory_space=pl.ANY), VM, VM, VM, VM],
-        out_specs=[VM, VM],
+        in_specs=[anywhere] * 8,
+        out_specs=[anywhere] * 2,
         out_shape=[jax.ShapeDtypeStruct((OWN, T, T), F32)] * 2,
         scratch_shapes=scratch,
         compiler_params=pltpu.CompilerParams(
             collective_id=0, has_side_effects=True, vmem_limit_bytes=LIMIT
         ),
         name="sweep",
-    )(by_row, by_col, v, tiles, in_row, in_col, audio_seeds, video_seeds)
+    )(by_row, by_col, in_row, in_col, v, tiles, audio_seeds, video_seeds)
 
 
 def turn_kernel(a, b, a_out, b_out):
@@ -554,10 +635,10 @@
     audio, video = sweep(
         by_row,
         by_col,
+        in_row,
+        in_col,
         video_scores_in.reshape(OWN, T, T),
         tile_values[0, 0],
-        in_row,
-        in_col,
         audio_seed.reshape(OWN, T),
         video_seed.reshape(OWN, T),
     )

time: 118 us -> 118 us (level)
  Pallas kernels: 113 us -> 117 us
  local copies, waits for them, and re-layouts: 3.88 us -> 0 us
    unnamed x12 -> x0, local copies, waits for them, and re-layouts: 3.88 us -> none
    pallas_call x2, Pallas kernels: 110 us -> 114 us  [the longest x1 111 us: sweep(): pl.pallas_call(sweep_kernel, in_specs=[anywhere] * 8, out_specs=[anywhere...]
where the time goes in v1:
time: 118 us
  Pallas kernels  117 us (99%)
  between operations  1.29 us (1%)
    pallas_call x1, Pallas kernels, sweep(): pl.pallas_call(sweep_kernel, in_specs=[anywhere] * 8, out_specs=[anywhere...  111 us
    pallas_call x1, Pallas kernels, plan(): pl.pallas_call(plan_kernel, in_specs=[anywhere] * 3, out_specs=[hbm] * 4,...  3.14 us
    pallas_call x1, Pallas kernels, turn(): pl.pallas_call(turn_kernel, in_specs=[VM, VM], out_specs=[VM, VM], out_sh...  2.5 us

profile of v1, /device:TPU:1, one launch (start us, length us, event | category | flops | bytes accessed | tf_op | source)
XLA Modules:
  0.0 117.9 jit_solution(8129701875775407671)
XLA Ops:
  1.3 3.1 %plan.1 = (s32[8,768]{1,0:T(8,128)}, s32[8,768]{1,0:T(8,128)}, bf16[128,640]{1,0:T(8,128)(2,1)}, bf16[64,640]{1,0:T(8,128)(2,1)}) custom-call(s32[1,1]{1,0:T(1,128)S(6)} %copy.9.count_in, s32[1,640]{1,0:T(1,128)} %bitcast.12, s32[1,640]{1,0:T(1,128)} %bitcast.13), custom_call_target="tpu_custom_call" | custom-call | tf_op jit(solution)/shard_map/plan/pallas_call | solution.py:132
  4.4 110.9 %sweep.1 = (f32[8,128,128]{2,1,0:T(8,128)}, f32[8,128,128]{2,1,0:T(8,128)}) custom-call(s32[8,768]{1,0:T(8,128)} %get-tuple-element.10.by_row_in, s32[8,768]{1,0:T(8,128)} %get-tuple-element.11.by_col_in, bf16[128,640]{1,0:T(8,128)(2,1)} %get-tuple-element.12.in_row_in, bf16[64,640]{1,0:T(8,128)(2,1)} %get-tuple-element.13.in_col_in, ...), custom_call_target="tpu_custom_call" | custom-call | tf_op jit(solution)/shard_map/sweep/pallas_call | solution.py:601
  115.4 2.5 %turn.1 = (f32[8,128,128]{2,1,0:T(8,128)}, f32[8,128,128]{2,1,0:T(8,128)}) custom-call(f32[8,128,128]{2,1,0:T(8,128)} %get-tuple-element.14.a, f32[8,128,128]{2,1,0:T(8,128)} %get-tuple-element.15.b), custom_call_target="tpu_custom_call" | custom-call | tf_op jit(solution)/shard_map/turn/pallas_call | solution.py:621

commit v2 on v1

--- a/solution.py
+++ b/solution.py
@@ -13,7 +13,8 @@
 QUART = OWN // 4
 T = 128
 CHUNK = 32
-UNROLL = 16
+AHEAD = 5
+UNROLL = 32
 LIMIT = 67043328
 DIRS = (0, 1)
 REL = (2, 1, 3, 0)
@@ -53,7 +54,7 @@
     barrier = pltpu.get_barrier_semaphore()
     for peer in peers:
         pl.semaphore_signal(barrier, inc=1, device_id=peer, device_id_type=MESH)
-    pl.semaphore_wait(barrier, len(peers))
+    return lambda: pl.semaphore_wait(barrier, len(peers))
 
 
 def sort_slots(count, rows, cols, by_row, by_col, in_row, in_col):
@@ -192,32 +193,36 @@
         copy.start()
         return copy
 
+    met = greet([peer(axis, d) for axis in "xyz" for d in DIRS] + [mate])
     v_load = local(v_in, v, 0)
+
+    def chunk(i):
+        span = pl.ds(i * CHUNK, CHUNK)
+        return pltpu.make_async_copy(tiles_in.at[span], tiles.at[span], load.at[i])
+
+    for i in range(AHEAD):
+        chunk(i).start()
     index_loads = [local(by_row_in, by_row, 1), local(by_col_in, by_col, 2)]
     member_loads = [local(in_row_in, in_row, 3), local(in_col_in, in_col, 6)]
     seed_loads = [local(audio_seeds_in, audio_seeds, 4), local(video_seeds_in, video_seeds, 5)]
-    loads = []
-    for i in range(n_chunks):
-        span = pl.ds(i * CHUNK, CHUNK)
-        copy = pltpu.make_async_copy(tiles_in.at[span], tiles.at[span], load.at[i])
-        copy.start()
-        loads.append(copy)
     tiles[slots] = jnp.zeros((T, T), BF16)
 
     v_load.wait()
     panel[pl.ds(row_id * OWN, OWN)] = v[...].astype(BF16)
-    greet([peer(axis, d) for axis in "xyz" for d in DIRS] + [mate])
-
-    def push_video(index, first, size, to):
-        ref = panel.at[pl.ds(index * OWN + first, size)]
+    met()
+
+    def push_video(index, d, to):
+        ref = panel.at[pl.ds(index * OWN + d * (OWN // 2), OWN // 2)]
         return start(ref, ref, to)
 
-    def tile_sums(chunks):
-        for i in chunks:
-            loads[i].wait()
-
-        @pl.loop(chunks[0], chunks[-1] + 1)
+    def tile_sums(first, last):
+        @pl.loop(first, last)
         def _(i):
+            @pl.when(i + AHEAD < n_chunks)
+            def _():
+                chunk(i + AHEAD).start()
+
+            chunk(i).wait()
             sums = lax.dot_general(
                 jnp.ones((8, T), BF16),
                 tiles[pl.ds(i * CHUNK, CHUNK)].reshape(CHUNK * T, T),
@@ -230,21 +235,21 @@
                     tiles[i * CHUNK + s].astype(F32), axis=0, keepdims=True
                 )
 
-    cut = (n_chunks * 7 // 20, n_chunks * 14 // 20)
-    hop = [push_video(row_id, 0, OWN, peer("z", d)) for d in DIRS]
-    mates = [push_video(row_id, 0, OWN, mate)]
-    tile_sums(range(0, cut[0]))
+    near = [peer("z", d) for d in DIRS]
+    origin = [at("z", step(1 - d)) * 2 + core for d in DIRS]
+    early = [push_video(row_id, d, near[d]) for d in DIRS]
+    late = [push_video(row_id, 1 - d, near[d]) for d in DIRS]
+    mates = [push_video(row_id, d, mate) for d in DIRS]
+    tile_sums(0, n_chunks // 2)
     far = []
     for d in DIRS:
-        index = at("z", step(1 - d)) * 2 + core
-        hop[d].wait_recv()
-        far.append(push_video(index, d * OWN // 2, OWN // 2, peer("z", d)))
-        mates.append(push_video(index, 0, OWN, mate))
-    tile_sums(range(cut[0], cut[1]))
+        early[d].wait_recv()
+        far.append(push_video(origin[d], d, near[d]))
+        mates.append(push_video(origin[d], d, mate))
+    tile_sums(n_chunks // 2, n_chunks)
     for d in DIRS:
-        far[d].wait_recv()
-        mates.append(push_video(at("z", 2) * 2 + core, d * OWN // 2, OWN // 2, mate))
-    tile_sums(range(cut[1], n_chunks))
+        late[d].wait_recv()
+        mates.append(push_video(origin[d], 1 - d, mate))
 
     def gathered(member, sums):
         value = sums[pl.ds(0, slots)]
@@ -262,6 +267,9 @@
     c_far = start(mass_in.at[:, at("x", 2)], mass_far, peer("x", 0))
     c_hop = start(mass_in.at[:, at("x", 3)], mass_hop.at[1], peer("x", 1))
     r_mate = start(mass_col.at[:, 1 - core], r_swap, mate)
+    for d in DIRS:
+        far[d].wait_recv()
+        mates.append(push_video(at("z", 2) * 2 + core, d, mate))
     for copy in index_loads:
         copy.wait()
     for copy in mates:
@@ -329,8 +337,9 @@
         held.shape[0],
         lambda t, c: tiles[t],
         lambda t, c: panel[c],
-        (mass_1, mass_2, mass_3),
+        (mass_1,),
     )
+    mass_2()
 
     @pl.loop(0, SIDE * SIDE)
     def _(o):
@@ -362,6 +371,7 @@
             axis = halves[h][0]
             c_opp[h, d, i] = start(cell(h, at(axis, 2), i, d), opp1.at[h, d, i], peer(axis, d))
     send_plain(0)
+    mass_3()
     for i in range(SIDE):
         for h, d in both:
             axis = halves[h][0]
@@ -540,7 +550,7 @@
     unit = (2, 2, SIDE, QUART, T, T)
     small = (2, 2, QUART, T, T)
     quad = (2, OWN // 2, T, T)
-    copies = 9 + 6 + 4 + 48 + 12 + 44 + 10
+    copies = 14 + 6 + 4 + 48 + 12 + 44 + 10
     scratch = [
         pltpu.VMEM((slots + 1, T, T), BF16),
         pltpu.VMEM((wide // 2, T, T), BF16),
@@ -611,18 +621,42 @@
     )(by_row, by_col, in_row, in_col, v, tiles, audio_seeds, video_seeds)
 
 
-def turn_kernel(a, b, a_out, b_out):
-    for t in range(OWN):
-        a_out[t] = a[t].T
-        b_out[t] = b[t].T
+def turn_kernel(a, b, a_out, b_out, before, after, load, store):
+    half = OWN // 2
+    moves = []
+    for i, (src, dst) in enumerate(((a, a_out), (b, b_out))):
+        for k in range(2):
+            span, n = pl.ds(k * half, half), 2 * i + k
+            moves.append(
+                (
+                    pltpu.make_async_copy(src.at[span], before.at[n], load.at[n]),
+                    pltpu.make_async_copy(after.at[n], dst.at[span], store.at[n]),
+                )
+            )
+            moves[-1][0].start()
+    for n, (come, go) in enumerate(moves):
+        come.wait()
+        for t in range(half):
+            after[n, t] = before[n, t].T
+        go.start()
+    for _, go in moves:
+        go.wait()
 
 
 def turn(a, b):
+    anywhere = pl.BlockSpec(memory_space=pl.ANY)
     return pl.pallas_call(
         turn_kernel,
-        in_specs=[VM, VM],
-        out_specs=[VM, VM],
+        in_specs=[anywhere] * 2,
+        out_specs=[anywhere] * 2,
         out_shape=[jax.ShapeDtypeStruct(a.shape, F32)] * 2,
+        scratch_shapes=[
+            pltpu.VMEM((4, OWN // 2, T, T), F32),
+            pltpu.VMEM((4, OWN // 2, T, T), F32),
+            pltpu.SemaphoreType.DMA((4,)),
+            pltpu.SemaphoreType.DMA((4,)),
+        ],
+        compiler_params=pltpu.CompilerParams(vmem_limit_bytes=LIMIT),
         name="turn",
     )(a, b)
 

time: 118 us -> 108 us (0.915)
  Pallas kernels: 117 us -> 107 us
    pallas_call x1, Pallas kernels: 111 us -> 101 us  [sweep(): pl.pallas_call(sweep_kernel, in_specs=[anywhere] * 8, out_specs=[anywhere...]
where the time goes in v2:
time: 108 us
  Pallas kernels  107 us (99%)
  between operations  1.29 us (1%)
    pallas_call x1, Pallas kernels, sweep(): pl.pallas_call(sweep_kernel, in_specs=[anywhere] * 8, out_specs=[anywhere...  101 us
    pallas_call x1, Pallas kernels, plan(): pl.pallas_call(plan_kernel, in_specs=[anywhere] * 3, out_specs=[hbm] * 4,...  3.14 us
    pallas_call x1, Pallas kernels, turn(): pl.pallas_call(turn_kernel, in_specs=[anywhere] * 2, out_specs=[anywhere]...  2.26 us

profile of v2, /device:TPU:1, one launch (start us, length us, event | category | flops | bytes accessed | tf_op | source)
XLA Modules:
  0.0 107.9 jit_solution(4461082601249656705)
XLA Ops:
  1.3 3.1 %plan.1 = (s32[8,768]{1,0:T(8,128)}, s32[8,768]{1,0:T(8,128)}, bf16[128,640]{1,0:T(8,128)(2,1)}, bf16[64,640]{1,0:T(8,128)(2,1)}) custom-call(s32[1,1]{1,0:T(1,128)S(6)} %copy.9.count_in, s32[1,640]{1,0:T(1,128)} %bitcast.12, s32[1,640]{1,0:T(1,128)} %bitcast.13), custom_call_target="tpu_custom_call" | custom-call | tf_op jit(solution)/shard_map/plan/pallas_call | solution.py:133
  4.4 101.2 %sweep.1 = (f32[8,128,128]{2,1,0:T(8,128)}, f32[8,128,128]{2,1,0:T(8,128)}) custom-call(s32[8,768]{1,0:T(8,128)} %get-tuple-element.10.by_row_in, s32[8,768]{1,0:T(8,128)} %get-tuple-element.11.by_col_in, bf16[128,640]{1,0:T(8,128)(2,1)} %get-tuple-element.12.in_row_in, bf16[64,640]{1,0:T(8,128)(2,1)} %get-tuple-element.13.in_col_in, ...), custom_call_target="tpu_custom_call" | custom-call | tf_op jit(solution)/shard_map/sweep/pallas_call | solution.py:611
  105.6 2.3 %turn.1 = (f32[8,128,128]{2,1,0:T(8,128)}, f32[8,128,128]{2,1,0:T(8,128)}) custom-call(f32[8,128,128]{2,1,0:T(8,128)} %get-tuple-element.14.a, f32[8,128,128]{2,1,0:T(8,128)} %get-tuple-element.15.b), custom_call_target="tpu_custom_call" | custom-call | tf_op jit(solution)/shard_map/turn/pallas_call | solution.py:648
